TPU v7x, 128 devices: a whole 4x4x4 slice. The times are simulated.
128 devices in a mesh: pair: 16 (over x, z_lo, core), aux: 8 (over y, z_hi).
Axes of the slice: x: 4, y: 4, z: 4 (z_hi: 2, z_lo: 2; z = z_hi * 2 + z_lo), core: 2. Of those that a mesh axis runs over, the one named last changes fastest.
Arguments:
- integrals: bfloat16 [16, 2, 512, 256, 256], P('pair', None, 'aux'), may hold values from -6 to 6
- coef_table: bfloat16 [2048, 2, 128], P('pair'), may hold values from -0.375 to 0.375
- row_slot: int32 [2048], replicated, may hold values from 0 to 2047, each once
- pair_k: int32 [16, 2], P('pair'), may hold values from 0 to 7, as said below
Outputs:
- exchange_k: float32 [2, 8, 256, 256], P(None, None, 'aux', 'pair')
Inputs may be any that keep to these rules, and one draw needn't show every extreme that they name: `row_slot`: each table row holds exactly one orbital row of one k-point. `pair_k`: the two k-points of a pair differ, and every k-point belongs to some listed pair.
All inputs are finite; a program needn't handle non-finite values.
Results may differ from a plain program's by a relative error of at most 0.0003.
Values may be sent and summed in bfloat16 or wider, within the bound.
A program may use at most 192 MiB of HBM per device.

v0:
```python
import jax
import jax.numpy as jnp
from jax import lax
from jax.sharding import PartitionSpec as P

NKPT = 8


def pick_rows(gathered, row_slot, kpoint, norbitals):
    slots = lax.dynamic_slice_in_dim(row_slot, kpoint * norbitals, norbitals)
    return gathered[slots].reshape(norbitals, -1)


def exchange_block(real_part, imag_part, factor):
    rounded_real = real_part.astype(jnp.bfloat16)
    rounded_imag = imag_part.astype(jnp.bfloat16)
    joined = jnp.concatenate([rounded_real, rounded_imag], -1)
    turned = jnp.concatenate([rounded_imag, -rounded_real], -1)
    k_real = jnp.einsum("pmj,plj->ml", joined, joined, preferred_element_type=jnp.float32)
    k_imag = jnp.einsum("pmj,plj->ml", turned, joined, preferred_element_type=jnp.float32)
    return jnp.stack([k_real, k_imag]) * factor


def local(integrals, coef_table, row_slot, pair_k):
    gathered = lax.all_gather(coef_table, "pair", axis=0, tiled=True)
    norbitals = integrals.shape[-1]
    noccupied = coef_table.shape[-1]
    factor = 1.0 / (integrals.shape[2] * lax.axis_size("aux") * noccupied)
    blocks = integrals[0]
    first_k = pair_k[0, 0]
    second_k = pair_k[0, 1]
    coeff_second = pick_rows(gathered, row_slot, second_k, norbitals)
    coeff_first = pick_rows(gathered, row_slot, first_k, norbitals)
    flat_blocks = blocks.reshape(-1, norbitals)
    product = jnp.dot(flat_blocks, coeff_second, preferred_element_type=jnp.float32)
    product = product.reshape(blocks.shape[:-1] + (2 * noccupied,))
    left_real = product[0, ..., :noccupied] - product[1, ..., noccupied:]
    left_imag = product[0, ..., noccupied:] + product[1, ..., :noccupied]
    first_block = exchange_block(left_real, left_imag, factor)
    product = jnp.einsum("cpmn,mj->cpnj", blocks, coeff_first, preferred_element_type=jnp.float32)
    right_real = product[0, ..., :noccupied] + product[1, ..., noccupied:]
    right_imag = product[0, ..., noccupied:] - product[1, ..., :noccupied]
    second_block = exchange_block(right_real, right_imag, factor)
    kpoints = jnp.arange(NKPT, dtype=jnp.int32)
    first_hot = (kpoints == first_k).astype(jnp.float32)[None, :, None, None]
    second_hot = (kpoints == second_k).astype(jnp.float32)[None, :, None, None]
    spread = first_block[:, None] * first_hot + second_block[:, None] * second_hot
    summed = lax.psum_scatter(spread, "pair", scatter_dimension=3, tiled=True)
    return lax.psum_scatter(summed, "aux", scatter_dimension=2, tiled=True)


def solution(mesh):
    in_specs = (P("pair", None, "aux", None, None), P("pair", None, None), P(), P("pair", None))
    out_specs = P(None, None, "aux", "pair")
    return jax.shard_map(local, mesh=mesh, in_specs=in_specs, out_specs=out_specs, check_vma=False)
```

profile of v0, /device:TPU:1, one launch (start us, length us, event | category | flops | bytes accessed | tf_op | source)
XLA Modules:
  0.0 332.0 jit_solution(5182410068761711925)
XLA Ops:
  6.5 0.0 all-gather.2.cloned.1.call-start
  6.5 0.7 all-gather.2.cloned.1.call-update
  7.3 0.0 reduce-scatter.5.cloned.1.call-start
  7.3 1.4 fusion.37
  10.0 1.3 compare_convert_fusion
  11.2 0.8 compare_select_fusion.1
  12.0 32.8 %all-gather.2.cloned.1.call-done = bf16[2048,2,128]{2,1,0:T(2,128)(2,1)} async-done(((bf16[128,2,128]{2,1,0:T(2,128)(2,1)}), bf16[2048,2,128]{2,1,0:T(2,128)(2,1)}) %all-gather.2.cloned.1.call-update) | async-done | bytes 1048592 | tf_op jit(solution)/shard_map/all_gather | solution.py:25
  44.8 2.2 gather_fusion.1
  47.0 0.1 copy.32
  47.1 18.9 %convolution_bitcast_fusion.1 = f32[2,64,256,256]{2,3,1,0:T(8,128)} fusion(bf16[256,256,1,1]{0,1,3,2:T(8,128)(2,1)S(1)} %bitcast.55, bf16[1,2,64,256,256]{4,3,2,1,0:T(8,128)(2,1)} %param.4), kind=kOutput, calls=%fused_computation.3 | convolution fusion | flops 4294967296 | bytes 50462720 | tf_op jit(solution)/shard_map/cpmn,mj->cpnj/dot_general | solution.py:40
  66.0 8.8 %fusion.18 = bf16[64,256,128]{1,2,0:T(8,128)(2,1)} fusion(f32[2,64,256,256]{2,3,1,0:T(8,128)} %convolution_bitcast_fusion.1), kind=kLoop, calls=%fused_computation.28 | loop fusion | flops 4194304 | bytes 20971520 | tf_op jit(solution)/shard_map/convert_element_type | solution.py:16
  74.8 9.8 %fusion.35 = (bf16[64,256,128]{1,2,0:T(8,128)(2,1)}, bf16[64,256,128]{1,2,0:T(8,128)(2,1)}) fusion(f32[2,64,256,256]{2,3,1,0:T(8,128)} %convolution_bitcast_fusion.1), kind=kLoop, calls=%fused_computation.49 | loop fusion | flops 6291456 | bytes 25165824 | tf_op jit(solution)/shard_map/neg | solution.py:18
  84.7 2.2 gather_fusion
  86.8 24.4 %convolution_bitcast_fusion = f32[32768,256]{0,1:T(8,128)} fusion(bf16[32768,256]{1,0:T(8,128)(2,1)} %bitcast.51, bf16[32,8,2,128]{3,2,1,0:T(2,128)(2,1)S(1)} %bitcast.53), kind=kOutput, calls=%fused_computation.2 | convolution fusion | flops 4294967296 | bytes 50462720 | tf_op jit(solution)/shard_map/dot_general | solution.py:35
  111.2 33.4 %copy.35 = f32[32768,256]{1,0:T(8,128)} copy(f32[32768,256]{0,1:T(8,128)} %convolution_bitcast_fusion) | data formatting | bytes 67108864 | tf_op jit(solution)/shard_map/reshape | solution.py:36
  144.6 8.6 %fusion.16 = bf16[64,256,128]{2,1,0:T(8,128)(2,1)} fusion(f32[2,64,256,256]{3,2,1,0:T(8,128)} %bitcast.49), kind=kLoop, calls=%fused_computation.26 | loop fusion | flops 4194304 | bytes 20971520 | tf_op jit(solution)/shard_map/convert_element_type | solution.py:16
  153.3 0.0 copy-start
  153.3 0.0 copy-start.3
  153.3 10.0 %fusion.33 = (bf16[64,256,128]{2,1,0:T(8,128)(2,1)}, bf16[64,256,128]{2,1,0:T(8,128)(2,1)}) fusion(f32[2,64,256,256]{3,2,1,0:T(8,128)} %bitcast.50), kind=kLoop, calls=%fused_computation.48 | loop fusion | flops 6291456 | bytes 25165824 | tf_op jit(solution)/shard_map/neg | solution.py:18
  163.3 0.0 copy-done
  163.3 1.4 copy-done.3
  164.6 0.0 copy-start.2
  164.6 2.4 fusion.20
  167.0 0.0 copy-done.2
  167.0 2.4 fusion.21
  169.4 0.2 copy.26
  169.6 0.0 copy-start.1
  169.6 0.0 copy-start.4
  169.6 0.0 copy-start.5
  169.6 8.4 %fusion.19 = f32[1,256,256]{2,1,0:T(8,128)S(1)} fusion(bf16[64,256,128]{2,1,0:T(8,128)(2,1)} %fusion.16, bf16[64,256,128]{2,1,0:T(8,128)(2,1)} %get-tuple-element.6), kind=kOutput, calls=%fused_computation.30 | convolution fusion | flops 2164260864 | bytes 8650752 | tf_op jit(solution)/shard_map/pmj,plj->ml/dot_general | solution.py:19
  178.0 0.0 copy-done.1
  178.0 0.0 copy-done.4
  178.0 1.1 copy-done.5
  179.1 2.4 fusion.24
  181.5 0.2 copy.20
  181.7 2.6 multiply_add_fusion
  184.3 0.0 reduce-scatter.5.cloned.1.call-update
  184.3 0.0 reduce-scatter.7.cloned.1.call-start
  184.4 64.5 %reduce-scatter.5.cloned.1.call-done = f32[2,8,256,16]{2,3,1,0:T(8,128)} async-done(((f32[2,8,256,256]{2,3,1,0:T(8,128)}), f32[2,8,256,16]{2,3,1,0:T(8,128)}) %reduce-scatter.5.cloned.1.call-update) | async-done | bytes 262160 | tf_op jit(solution)/shard_map/reduce_scatter | solution.py:48
  248.9 2.2 copy.33
  251.2 1.5 reshape.87
  252.7 0.0 reduce-scatter.7.cloned.1.call-update
  252.7 71.0 %reduce-scatter.7.cloned.1.call-done = f32[32,256]{1,0:T(8,128)} async-done(((f32[256,256]{1,0:T(8,128)}), f32[32,256]{1,0:T(8,128)}) %reduce-scatter.7.cloned.1.call-update) | async-done | bytes 32784
  323.7 0.9 reshape.88
  324.6 0.8 copy.34
  (3 shorter events, 0.1 us)
Async XLA Ops:
  6.5 38.3 %all-gather.2.cloned.1.call-start = ((), (), s32[]{:S(2)}) async-start(), calls=%async_computation.2 | async-start | bytes 1114112 | tf_op jit(solution)/shard_map/all_gather | solution.py:25
  7.3 241.7 %reduce-scatter.5.cloned.1.call-start = ((), (), s32[]{:S(2)}) async-start(), calls=%async_computation.3 | async-start | bytes 4456448 | tf_op jit(solution)/shard_map/reduce_scatter | solution.py:48
  153.3 10.0 %copy-start = (bf16[64,256,128]{1,2,0:T(8,128)(2,1)S(1)}, bf16[64,256,128]{1,2,0:T(8,128)(2,1)}, u32[]{:S(2)}) copy-start(bf16[64,256,128]{1,2,0:T(8,128)(2,1)} %fusion.18) | copy-start | bytes 12582916
  153.3 11.3 %copy-start.3 = (bf16[64,256,128]{1,2,0:T(8,128)(2,1)S(1)}, bf16[64,256,128]{1,2,0:T(8,128)(2,1)}, u32[]{:S(2)}) copy-start(bf16[64,256,128]{1,2,0:T(8,128)(2,1)} %get-tuple-element.8) | copy-start | bytes 12582916
  164.6 2.4 copy-start.2
  169.6 8.4 %copy-start.1 = (bf16[64,256,128]{2,1,0:T(8,128)(2,1)S(1)}, bf16[64,256,128]{2,1,0:T(8,128)(2,1)}, u32[]{:S(2)}) copy-start(bf16[64,256,128]{2,1,0:T(8,128)(2,1)} %fusion.16) | copy-start | bytes 12582916
  169.6 8.4 %copy-start.4 = (bf16[64,256,128]{2,1,0:T(8,128)(2,1)S(1)}, bf16[64,256,128]{2,1,0:T(8,128)(2,1)}, u32[]{:S(2)}) copy-start(bf16[64,256,128]{2,1,0:T(8,128)(2,1)} %get-tuple-element.5) | copy-start | bytes 12582916
  169.6 9.5 %copy-start.5 = (bf16[64,256,128]{2,1,0:T(8,128)(2,1)S(1)}, bf16[64,256,128]{2,1,0:T(8,128)(2,1)}, u32[]{:S(2)}) copy-start(bf16[64,256,128]{2,1,0:T(8,128)(2,1)} %get-tuple-element.6) | copy-start | bytes 12582916
  184.3 139.4 %reduce-scatter.7.cloned.1.call-start = ((), (), s32[]{:S(2)}) async-start(), calls=%async_computation.4 | async-start | bytes 294912
Sparse Core Ops, SparseCore 0:
  9.0 35.7 all-gather.1
  184.5 64.4 reduce-scatter.4
  252.8 70.8 reduce-scatter.6
where the time goes:
time: 334 us; the launch traced here: 332 us
  waiting for transfers between devices  169 us (51%)
  matrix products  58.8 us (18%)
  local copies, waits for them, and re-layouts  47.5 us (14%)
  other arithmetic  41.9 us (13%)
  between operations  14.6 us (4%)
    unnamed x4, waiting for transfers between devices  71.8 us
    reduce_scatter x1, waiting for transfers between devices, local(): summed = lax.psum_scatter(spread, 'pair', scatter_dimension=3, tiled=True)  64.5 us
    reshape x1, local copies, waits for them, and re-layouts, local(): product = product.reshape(blocks.shape[:-1] + (2 * noccupied,))  33.4 us
    all_gather x1, waiting for transfers between devices, local(): gathered = lax.all_gather(coef_table, 'pair', axis=0, tiled=True)  32.8 us
    dot_general x1, matrix products, local(): jnp.dot(flat_blocks, coeff_second, preferred_element_type=jnp.float32)  24.4 us
    neg x2, other arithmetic, exchange_block(): turned = jnp.concatenate([rounded_imag, -rounded_real], -1)  19.8 us
    dot_general x1, matrix products, local(): jnp.einsum('cpmn,mj->cpnj', blocks, coeff_first, preferred_element_type=j...  18.9 us
    convert_element_type x2, other arithmetic, exchange_block(): rounded_imag = imag_part.astype(jnp.bfloat16)  17.4 us
  transfers between devices with their start and end apart: 3, of which 3 were waited for; matrix products, arithmetic and copies ran while one was open for 1% of the time, Pallas kernels for 0%

commit v1 on v0

v1 whole, which is shorter than its diff:
```python
import jax
import jax.numpy as jnp
from jax import lax
from jax.experimental import pallas as pl
from jax.experimental.pallas import tpu as pltpu
from jax.sharding import PartitionSpec as P

NKPT = 8
NORB = 256
NOCC = 128
NPAIR = 16
NSLAB = 8
ROWS = 128
PIECE = 144
GROUP = 16
CHUNKS = 16
F32 = jnp.float32
BF16 = jnp.bfloat16
MESH = pl.DeviceIdType.MESH


def product(left, right):
    return lax.dot_general(left, right, (((1,), (0,)), ((), ())), preferred_element_type=F32)


def product_nt(left, right):
    return lax.dot_general(left, right, (((1,), (1,)), ((), ())), preferred_element_type=F32)


def product_tn(left, right):
    return lax.dot_general(left, right, (((0,), (0,)), ((), ())), preferred_element_type=F32)


def kernel(pair_ref, piece_ref, slot_ref, blocks_ref, out_ref, blocks, table, picked, first_w, second_w,
           k_real, k_cross, sums_out, sums_in, tiles_out, tiles_in,
           load_sem, table_send, table_recv, sums_send, sums_recv, tiles_send, tiles_recv):
    me = lax.axis_index("pair")
    slab = lax.axis_index("aux")
    naux = blocks.shape[1]
    step = naux // CHUNKS
    factor = 1.0 / (naux * NSLAB * NOCC)

    def load(chunk):
        span = pl.ds(chunk * step, step)
        return pltpu.make_async_copy(blocks_ref.at[:, span], blocks.at[:, span], load_sem.at[chunk])

    for chunk in range(CHUNKS):
        load(chunk).start()

    barrier = pltpu.get_barrier_semaphore()
    for offset in range(1, NPAIR):
        pl.semaphore_signal(barrier, inc=1, device_id=(lax.rem(me + offset, NPAIR), slab), device_id_type=MESH)
    for offset in range(1, NSLAB):
        pl.semaphore_signal(barrier, inc=1, device_id=(me, lax.rem(slab + offset, NSLAB)), device_id_type=MESH)

    first_k = pair_ref[0, 0]
    second_k = pair_ref[0, 1]
    slots = slot_ref[...]
    columns = []
    for kpoint in (second_k, first_k):
        for half in range(2):
            row = jnp.zeros((1, ROWS), jnp.int32)
            for k in range(NKPT):
                row = jnp.where(kpoint == k, slots[2 * k + half:2 * k + half + 1], row)
            columns.append(jnp.broadcast_to(row, (ROWS, ROWS)).T)
    wanted = jnp.concatenate(columns, 0)
    lane = lax.broadcasted_iota(jnp.int32, wanted.shape, 1)

    pl.semaphore_wait(barrier, NPAIR + NSLAB - 2)

    def table_copy(offset):
        return pltpu.make_async_remote_copy(
            src_ref=piece_ref, dst_ref=table.at[me], send_sem=table_send.at[offset], recv_sem=table_recv.at[offset],
            device_id=(lax.rem(me + offset, NPAIR), slab), device_id_type=MESH)

    for offset in range(1, NPAIR):
        table_copy(offset).start()
    table[me] = piece_ref[...]

    for offset in range(NPAIR):
        owner = lax.rem(me + NPAIR - offset, NPAIR)
        if offset:
            table_copy(offset).wait_recv()
        hot = jnp.where(wanted == owner * ROWS + lane, 1.0, 0.0).astype(BF16)
        term = product(hot, table[owner, :ROWS])
        if offset:
            picked[...] += term
        else:
            picked[...] = term

    for at, ref in ((0, second_w), (NORB, first_w)):
        real = picked[at:at + NORB, :NOCC]
        imag = picked[at:at + NORB, NOCC:]
        if ref is second_w:
            ref[...] = jnp.concatenate(
                [jnp.concatenate([real, imag], 1), jnp.concatenate([-imag, real], 1)], 0).astype(BF16)
        else:
            ref[...] = jnp.concatenate(
                [jnp.concatenate([real, imag], 1).T, jnp.concatenate([imag, -real], 1).T], 1).astype(BF16)

    def sums_copy(block, offset):
        peer = lax.rem(slab + offset, NSLAB)
        return pltpu.make_async_remote_copy(
            src_ref=sums_out.at[block, peer], dst_ref=sums_in.at[block, slab],
            send_sem=sums_send.at[block, offset], recv_sem=sums_recv.at[block, offset],
            device_id=(me, peer), device_id_type=MESH)

    def clear():
        k_real[...] = jnp.zeros_like(k_real)
        k_cross[...] = jnp.zeros_like(k_cross)

    def send_sums(block):
        cross = k_cross[...]
        parts = (k_real[...] * factor, (cross.T - cross) * factor)
        at = lax.broadcasted_iota(jnp.int32, (ROWS, ROWS), 1)
        for peer in range(NSLAB):
            tile, shift = peer // 4, peer % 4 * 32
            message = None
            for half in range(2):
                for part in range(2):
                    begin = half * 64 + part * 32
                    value = parts[part][half * ROWS:(half + 1) * ROWS, tile * ROWS:(tile + 1) * ROWS]
                    turn = (begin - shift) % ROWS
                    if turn:
                        value = pltpu.roll(value, turn, 1)
                    message = value if message is None else jnp.where(at >= begin, value, message)
            sums_out[block, peer] = message
        for offset in range(1, NSLAB):
            sums_copy(block, offset).start()

    clear()

    def left(group, carry):
        for chunk in range(GROUP // step):
            load(group * (GROUP // step) + chunk).wait()
        rounded = []
        for p in range(GROUP):
            both = jnp.concatenate([blocks[0, group * GROUP + p], blocks[1, group * GROUP + p]], 1)
            rounded.append(product(both, second_w[...]).astype(BF16))
        real = jnp.concatenate([x[:, :NOCC] for x in rounded], 1)
        imag = jnp.concatenate([x[:, NOCC:] for x in rounded], 1)
        terms = product_nt(jnp.concatenate([real, imag], 0), real)
        k_real[...] += terms[:NORB] + product_nt(imag, imag)
        k_cross[...] += terms[NORB:]
        return carry

    lax.fori_loop(0, naux // GROUP, left, 0)
    send_sums(0)
    clear()

    def right(group, carry):
        rounded = []
        for p in range(GROUP):
            both = jnp.concatenate([blocks[0, group * GROUP + p], blocks[1, group * GROUP + p]], 0)
            rounded.append(product(first_w[...], both).astype(BF16))
        real = jnp.concatenate([x[:NOCC] for x in rounded], 0)
        imag = jnp.concatenate([x[NOCC:] for x in rounded], 0)
        terms = product_tn(jnp.concatenate([real, imag], 1), real)
        k_real[...] += terms[:NORB] + product_tn(imag, imag)
        k_cross[...] += terms[NORB:]
        return carry

    lax.fori_loop(0, naux // GROUP, right, 0)
    send_sums(1)

    low = lax.broadcasted_iota(jnp.int32, (ROWS, ROWS), 1) < 64
    totals = []
    for block in range(2):
        sums_in[block, slab] = sums_out[block, slab]
        for offset in range(1, NSLAB):
            sums_copy(block, offset).wait_recv()
        total = sums_in[block, 0]
        for sender in range(1, NSLAB):
            total = total + sums_in[block, sender]
        totals.append(total)
    tiles_out[:ROWS] = jnp.where(low, totals[0], pltpu.roll(totals[1], 64, 1))
    tiles_out[ROWS:] = jnp.where(low, pltpu.roll(totals[0], 64, 1), totals[1])

    def tile_copy(offset):
        peer = lax.rem(me + offset, NPAIR)
        return pltpu.make_async_remote_copy(
            src_ref=tiles_out.at[pl.ds(pl.multiple_of(peer * 16, 16), 16)], dst_ref=tiles_in.at[me],
            send_sem=tiles_send.at[offset], recv_sem=tiles_recv.at[offset],
            device_id=(peer, slab), device_id_type=MESH)

    for offset in range(1, NPAIR):
        tile_copy(offset).start()
    tiles_in[me] = tiles_out[pl.ds(pl.multiple_of(me * 16, 16), 16)]
    for offset in range(1, NPAIR):
        tile_copy(offset).wait_recv()
    kept = [jnp.zeros((16, ROWS), F32) for k in range(NKPT)]
    for owner in range(NPAIR):
        kpoint = table[owner, ROWS:PIECE, :ROWS].astype(F32)
        tile = tiles_in[owner]
        kept = [kept[k] + jnp.where(kpoint == k, tile, 0.0) for k in range(NKPT)]
    kept = [value + pltpu.roll(value, 64, 1) for value in kept]
    out_ref[...] = jnp.concatenate(kept, 0).T[:64]

    for offset in range(1, NPAIR):
        table_copy(offset).wait_send()
        tile_copy(offset).wait_send()
    for offset in range(1, NSLAB):
        sums_copy(0, offset).wait_send()
        sums_copy(1, offset).wait_send()


def local(integrals, coef_table, row_slot, pair_k):
    naux = integrals.shape[2]
    blocks = integrals.reshape(integrals.shape[1:])
    kpoints = jnp.repeat(pair_k.astype(BF16), 64, axis=1)
    kpoints = jnp.broadcast_to(jnp.concatenate([kpoints, kpoints], 1), (PIECE - ROWS, NORB))
    piece = jnp.concatenate([coef_table.reshape(ROWS, 2 * NOCC), kpoints], 0)
    vmem = pl.BlockSpec(memory_space=pltpu.VMEM)
    out = pl.pallas_call(
        kernel,
        out_shape=jax.ShapeDtypeStruct((64, ROWS), F32),
        in_specs=[pl.BlockSpec(memory_space=pltpu.SMEM), vmem, vmem, pl.BlockSpec(memory_space=pl.ANY)],
        out_specs=vmem,
        scratch_shapes=[
            pltpu.VMEM((2, naux, NORB, NORB), BF16),
            pltpu.VMEM((NPAIR, PIECE, NORB), BF16),
            pltpu.VMEM((2 * NORB, NORB), F32),
            pltpu.VMEM((NORB, 2 * NORB), BF16),
            pltpu.VMEM((2 * NORB, NORB), BF16),
            pltpu.VMEM((NORB, NORB), F32),
            pltpu.VMEM((NORB, NORB), F32),
            pltpu.VMEM((2, NSLAB, ROWS, ROWS), F32),
            pltpu.VMEM((2, NSLAB, ROWS, ROWS), F32),
            pltpu.VMEM((NORB, ROWS), F32),
            pltpu.VMEM((NPAIR, 16, ROWS), F32),
            pltpu.SemaphoreType.DMA((CHUNKS,)),
            pltpu.SemaphoreType.DMA((NPAIR,)),
            pltpu.SemaphoreType.DMA((NPAIR,)),
            pltpu.SemaphoreType.DMA((2, NSLAB)),
            pltpu.SemaphoreType.DMA((2, NSLAB)),
            pltpu.SemaphoreType.DMA((NPAIR,)),
            pltpu.SemaphoreType.DMA((NPAIR,)),
        ],
        compiler_params=pltpu.CompilerParams(
            collective_id=0, has_side_effects=True, vmem_limit_bytes=56 * 2**20),
    )(pair_k, piece, row_slot.reshape(16, ROWS), blocks)
    return out.reshape(2, 32, NKPT, 16).transpose(0, 2, 1, 3)


def solution(mesh):
    in_specs = (P("pair", None, "aux", None, None), P("pair", None, None), P(), P("pair", None))
    out_specs = P(None, None, "aux", "pair")
    return jax.shard_map(local, mesh=mesh, in_specs=in_specs, out_specs=out_specs, check_vma=False)
```

time: 334 us -> 66.8 us (0.20)
  waiting for transfers between devices: 169 us -> 0 us
  Pallas kernels: 0 us -> 62.5 us
  matrix products: 58.8 us -> 0 us
  local copies, waits for them, and re-layouts: 47.5 us -> 2.66 us
  other arithmetic: 41.9 us -> 1.32 us
  between operations: 14.6 us -> 0.03 us
    unnamed x4 -> x0, waiting for transfers between devices: 71.8 us -> none
    reduce_scatter x1 -> x0, waiting for transfers between devices: 64.5 us -> none  [local(): summed = lax.psum_scatter(spread, 'pair', scatter_dimension=3, tiled=True)]
    pallas_call x0 -> x1, Pallas kernels: none -> 62.5 us  [local(): pl.pallas_call(kernel, out_shape=jax.ShapeDtypeStruct((64, ROWS), F32), i...]
    dot_general x6 -> x0, matrix products: 58.8 us -> none  [the longest x1 24.4 us: local(): jnp.dot(flat_blocks, coeff_second, preferred_element_type=jnp.float32)]
    reshape x2 -> x1, local copies, waits for them, and re-layouts: 33.5 us -> 0.13 us  [local(): return out.reshape(2, 32, NKPT, 16).transpose(0, 2, 1, 3)]
    all_gather x1 -> x0, waiting for transfers between devices: 32.8 us -> none  [local(): gathered = lax.all_gather(coef_table, 'pair', axis=0, tiled=True)]
    neg x2 -> x0, other arithmetic: 19.8 us -> none  [exchange_block(): turned = jnp.concatenate([rounded_imag, -rounded_real], -1)]
    convert_element_type x3 -> x1, other arithmetic: 18.7 us -> 0.66 us  [local(): kpoints = jnp.repeat(pair_k.astype(BF16), 64, axis=1)]
  transfers between devices with their start and end apart: 3 -> 0, of which waited for: 3 -> 0; matrix products, arithmetic and copies ran while one was open for 1% -> 0% of each run, Pallas kernels for 0% -> 0%
where the time goes in v1:
time: 66.8 us; the launch traced here: 66.6 us
  Pallas kernels  62.5 us (94%)
  local copies, waits for them, and re-layouts  2.66 us (4%)
  other arithmetic  1.32 us (2%)
    pallas_call x1, Pallas kernels, local(): pl.pallas_call(kernel, out_shape=jax.ShapeDtypeStruct((64, ROWS), F32), i...  62.5 us

profile of v1, /device:TPU:1, one launch (start us, length us, event | category | flops | bytes accessed | tf_op | source)
XLA Modules:
  0.0 66.6 jit_solution(6489795282960839414)
XLA Ops:
  0.0 0.7 convert_bitcast_fusion
  0.7 0.1 broadcast_in_dim.12
  0.7 0.1 broadcast_in_dim.13
  0.9 0.8 %copy.10 = bf16[16,8,2,128]{3,1,2,0:T(8,128)(2,1)S(1)} copy(bf16[16,8,2,128]{3,2,1,0:T(2,128)(2,1)} %bitcast.14) | data formatting | bytes 131072
  1.7 0.6 pad_maximum_fusion.piece_ref
  2.3 62.5 %shard_map.46 = f32[64,128]{1,0:T(8,128)} custom-call(s32[1,2]{1,0:T(1,128)} %pair_ref.1, bf16[144,256]{1,0:T(8,128)(2,1)} %pad_maximum_fusion.piece_ref, s32[16,128]{1,0:T(8,128)} %bitcast.15, bf16[2,64,256,256]{3,2,1,0:T(8,128)(2,1)} %bitcast.11), custom_call_target="tpu_custom_call" | custom-call | tf_op jit(solution)/shard_map/pallas_call | solution.py:214
  64.9 0.8 %copy.6 = f32[64,128]{0,1:T(8,128)S(1)} copy(f32[64,128]{1,0:T(8,128)} %shard_map.46) | data formatting | bytes 65536 | tf_op jit(solution)/shard_map/pallas_call | solution.py:214
  65.8 0.1 reshape.20
  65.9 0.7 copy.7
  (2 shorter events, 0.0 us)

commit v2 on v1

--- a/solution.py
+++ b/solution.py
@@ -11,7 +11,7 @@
 NPAIR = 16
 NSLAB = 8
 ROWS = 128
-PIECE = 144
+HALVES = 2
 GROUP = 16
 CHUNKS = 16
 F32 = jnp.float32
@@ -31,7 +31,20 @@
     return lax.dot_general(left, right, (((0,), (0,)), ((), ())), preferred_element_type=F32)
 
 
-def kernel(pair_ref, piece_ref, slot_ref, blocks_ref, out_ref, blocks, table, picked, first_w, second_w,
+def neighbours(me, slab):
+    x, low, core = me // 4, me // 2 % 2, me % 2
+    y, high = slab // 2, slab % 2
+    across = x * 4 + (1 - low) * 2 + core
+    return {
+        "x+": (lax.rem(x + 1, 4) * 4 + low * 2 + core, slab),
+        "x-": (lax.rem(x + 3, 4) * 4 + low * 2 + core, slab),
+        "z+": (across, y * 2 + lax.rem(high + low, 2)),
+        "z-": (across, y * 2 + lax.rem(high + 1 - low, 2)),
+        "core": (me + 1 - 2 * core, slab),
+    }
+
+
+def kernel(pair_ref, piece_ref, slot_ref, blocks_ref, out_ref, blocks, table, offsets, picked, first_w, second_w,
            k_real, k_cross, sums_out, sums_in, tiles_out, tiles_in,
            load_sem, table_send, table_recv, sums_send, sums_recv, tiles_send, tiles_recv):
     me = lax.axis_index("pair")
@@ -39,64 +52,151 @@
     naux = blocks.shape[1]
     step = naux // CHUNKS
     factor = 1.0 / (naux * NSLAB * NOCC)
+    peers = neighbours(me, slab)
 
     def load(chunk):
         span = pl.ds(chunk * step, step)
         return pltpu.make_async_copy(blocks_ref.at[:, span], blocks.at[:, span], load_sem.at[chunk])
 
+    barrier = pltpu.get_barrier_semaphore()
+    greeted = [peers["z+"], peers["z-"]]
+    greeted += [(lax.rem(me + offset, NPAIR), slab) for offset in range(1, NPAIR)]
+    greeted += [(me, lax.rem(slab + offset, NSLAB)) for offset in range(1, NSLAB)]
+    for peer in greeted:
+        pl.semaphore_signal(barrier, inc=1, device_id=peer, device_id_type=MESH)
+
     for chunk in range(CHUNKS):
         load(chunk).start()
-
-    barrier = pltpu.get_barrier_semaphore()
-    for offset in range(1, NPAIR):
-        pl.semaphore_signal(barrier, inc=1, device_id=(lax.rem(me + offset, NPAIR), slab), device_id_type=MESH)
-    for offset in range(1, NSLAB):
-        pl.semaphore_signal(barrier, inc=1, device_id=(me, lax.rem(slab + offset, NSLAB)), device_id_type=MESH)
 
     first_k = pair_ref[0, 0]
     second_k = pair_ref[0, 1]
     slots = slot_ref[...]
-    columns = []
-    for kpoint in (second_k, first_k):
+    lane = lax.broadcasted_iota(jnp.int32, (ROWS, ROWS), 1)
+    for at, kpoint in enumerate((second_k, first_k)):
         for half in range(2):
             row = jnp.zeros((1, ROWS), jnp.int32)
             for k in range(NKPT):
                 row = jnp.where(kpoint == k, slots[2 * k + half:2 * k + half + 1], row)
-            columns.append(jnp.broadcast_to(row, (ROWS, ROWS)).T)
-    wanted = jnp.concatenate(columns, 0)
-    lane = lax.broadcasted_iota(jnp.int32, wanted.shape, 1)
-
-    pl.semaphore_wait(barrier, NPAIR + NSLAB - 2)
-
-    def table_copy(offset):
+            place = 2 * jnp.broadcast_to(row, (ROWS, ROWS)).T - lane
+            for part in range(2):
+                begin = (at * 4 + part * 2 + half) * ROWS
+                offsets[begin:begin + ROWS] = place + part
+
+    pl.semaphore_wait(barrier, len(greeted))
+
+    low_z, core = me // 2 % 2, me % 2
+    x = me // 4
+    own = {(dx, dz): lax.rem(x + dx, 4) * 4 + (low_z if dz == 0 else 1 - low_z) * 2 + core
+           for dx in range(4) for dz in range(2)}
+    lanes_of = {}
+
+    def table_copy(source, half, peer):
+        key = (source, half, peer)
+        at = lanes_of.setdefault(key, len(lanes_of))
+        slot = own[source]
+        origin = piece_ref.at[half] if source == (0, 0) else table.at[slot, half]
         return pltpu.make_async_remote_copy(
-            src_ref=piece_ref, dst_ref=table.at[me], send_sem=table_send.at[offset], recv_sem=table_recv.at[offset],
-            device_id=(lax.rem(me + offset, NPAIR), slab), device_id_type=MESH)
-
-    for offset in range(1, NPAIR):
-        table_copy(offset).start()
-    table[me] = piece_ref[...]
-
-    for offset in range(NPAIR):
-        owner = lax.rem(me + NPAIR - offset, NPAIR)
-        if offset:
-            table_copy(offset).wait_recv()
-        hot = jnp.where(wanted == owner * ROWS + lane, 1.0, 0.0).astype(BF16)
-        term = product(hot, table[owner, :ROWS])
-        if offset:
-            picked[...] += term
-        else:
-            picked[...] = term
-
-    for at, ref in ((0, second_w), (NORB, first_w)):
-        real = picked[at:at + NORB, :NOCC]
-        imag = picked[at:at + NORB, NOCC:]
-        if ref is second_w:
-            ref[...] = jnp.concatenate(
-                [jnp.concatenate([real, imag], 1), jnp.concatenate([-imag, real], 1)], 0).astype(BF16)
-        else:
-            ref[...] = jnp.concatenate(
-                [jnp.concatenate([real, imag], 1).T, jnp.concatenate([imag, -real], 1).T], 1).astype(BF16)
+            src_ref=origin, dst_ref=table.at[slot, half], send_sem=table_send.at[at], recv_sem=table_recv.at[at],
+            device_id=peers[peer], device_id_type=MESH)
+
+    sent = []
+
+    def send(source, half, peer):
+        copy = table_copy(source, half, peer)
+        copy.start()
+        sent.append(copy)
+
+    def arrive(source, half, peer):
+        dx, dz = source
+        if peer[0] == "x":
+            dx = (dx + (1 if peer == "x+" else 3)) % 4
+        if peer[0] == "z":
+            dz = 1 - dz
+        table_copy((dx, dz), half, peer).wait_recv()
+
+    def pick(slot, source=None):
+        rows = table[slot].reshape(2 * ROWS, ROWS) if source is None else source
+        base = slot * (2 * ROWS)
+        hot = [jnp.where(offsets[...] == base + half * ROWS, 1.0, 0.0).astype(BF16) for half in range(HALVES)]
+        return product(jnp.concatenate(hot, 1), rows)
+
+    def other(slot):
+        return slot + 1 - 2 * core
+
+    def from_core(source):
+        for half in range(HALVES):
+            at = lanes_of[(source, half, "core")]
+            slot = other(own[source])
+            pltpu.make_async_remote_copy(
+                src_ref=table.at[slot, half], dst_ref=table.at[slot, half],
+                send_sem=table_send.at[at], recv_sem=table_recv.at[at],
+                device_id=peers["core"], device_id_type=MESH).wait_recv()
+
+    HERE, LEFT, RIGHT, FAR = (0, 0), (3, 0), (1, 0), (2, 0)
+    send(HERE, 0, "x+")
+    send(HERE, 1, "x-")
+    send(HERE, 0, "z+")
+    send(HERE, 1, "z-")
+    send(HERE, 1, "x+")
+    send(HERE, 0, "x-")
+    send(HERE, 0, "core")
+    send(HERE, 1, "core")
+    picked[...] = pick(me, piece_ref[...].reshape(2 * ROWS, ROWS))
+    arrive(LEFT, 0, "x+")
+    send(LEFT, 0, "x+")
+    send(LEFT, 0, "z+")
+    send(LEFT, 0, "core")
+    arrive(RIGHT, 1, "x-")
+    send(RIGHT, 1, "x-")
+    send(RIGHT, 1, "z-")
+    send(RIGHT, 1, "core")
+    arrive((0, 1), 0, "z+")
+    send((0, 1), 0, "core")
+    arrive((0, 1), 1, "z-")
+    send((0, 1), 1, "core")
+    arrive(LEFT, 1, "x+")
+    send(LEFT, 1, "z+")
+    send(LEFT, 1, "core")
+    arrive(RIGHT, 0, "x-")
+    send(RIGHT, 0, "z-")
+    send(RIGHT, 0, "core")
+    for source in (LEFT, RIGHT, (0, 1)):
+        picked[...] += pick(own[source])
+    from_core(HERE)
+    picked[...] += pick(other(me))
+    arrive(FAR, 0, "x+")
+    send(FAR, 0, "z+")
+    send(FAR, 0, "core")
+    arrive(FAR, 1, "x-")
+    send(FAR, 1, "z-")
+    send(FAR, 1, "core")
+    picked[...] += pick(own[FAR])
+    for source, peer in (((3, 1), "z+"), ((1, 1), "z-")):
+        for half in range(HALVES):
+            arrive(source, half, peer)
+            send(source, half, "core")
+        picked[...] += pick(own[source])
+    for source in (LEFT, RIGHT, (0, 1), FAR):
+        from_core(source)
+        picked[...] += pick(other(own[source]))
+    arrive((2, 1), 0, "z+")
+    send((2, 1), 0, "core")
+    arrive((2, 1), 1, "z-")
+    send((2, 1), 1, "core")
+    for source in ((3, 1), (1, 1)):
+        from_core(source)
+        picked[...] += pick(other(own[source]))
+    picked[...] += pick(own[(2, 1)])
+    from_core((2, 1))
+    picked[...] += pick(other(own[(2, 1)]))
+
+    parts = [picked[begin:begin + NORB] for begin in range(0, 4 * NORB, NORB)]
+    real, imag = parts[:2]
+    second_w[...] = jnp.concatenate(
+        [jnp.concatenate([real, imag], 1), jnp.concatenate([-imag, real], 1)], 0).astype(BF16)
+    real, imag = parts[2:]
+    first_w[...] = jnp.concatenate(
+        [jnp.concatenate([real, imag], 1).T, jnp.concatenate([imag, -real], 1).T], 1).astype(BF16)
 
     def sums_copy(block, offset):
         peer = lax.rem(slab + offset, NSLAB)
@@ -164,6 +264,8 @@
     send_sums(1)
 
     low = lax.broadcasted_iota(jnp.int32, (ROWS, ROWS), 1) < 64
+    tiles_out[:, 16:] = jnp.broadcast_to(
+        jnp.where(low[:1], first_k, second_k).astype(F32), (NPAIR, 8, ROWS))
     totals = []
     for block in range(2):
         sums_in[block, slab] = sums_out[block, slab]
@@ -173,31 +275,34 @@
         for sender in range(1, NSLAB):
             total = total + sums_in[block, sender]
         totals.append(total)
-    tiles_out[:ROWS] = jnp.where(low, totals[0], pltpu.roll(totals[1], 64, 1))
-    tiles_out[ROWS:] = jnp.where(low, pltpu.roll(totals[0], 64, 1), totals[1])
+    tiles_out[:8, :16] = jnp.where(low, totals[0], pltpu.roll(totals[1], 64, 1)).reshape(8, 16, ROWS)
+    tiles_out[8:, :16] = jnp.where(low, pltpu.roll(totals[0], 64, 1), totals[1]).reshape(8, 16, ROWS)
 
     def tile_copy(offset):
         peer = lax.rem(me + offset, NPAIR)
         return pltpu.make_async_remote_copy(
-            src_ref=tiles_out.at[pl.ds(pl.multiple_of(peer * 16, 16), 16)], dst_ref=tiles_in.at[me],
+            src_ref=tiles_out.at[peer], dst_ref=tiles_in.at[me],
             send_sem=tiles_send.at[offset], recv_sem=tiles_recv.at[offset],
             device_id=(peer, slab), device_id_type=MESH)
 
     for offset in range(1, NPAIR):
         tile_copy(offset).start()
-    tiles_in[me] = tiles_out[pl.ds(pl.multiple_of(me * 16, 16), 16)]
+    tiles_in[me] = tiles_out[me]
     for offset in range(1, NPAIR):
         tile_copy(offset).wait_recv()
     kept = [jnp.zeros((16, ROWS), F32) for k in range(NKPT)]
     for owner in range(NPAIR):
-        kpoint = table[owner, ROWS:PIECE, :ROWS].astype(F32)
-        tile = tiles_in[owner]
+        tile = tiles_in[owner, :16]
+        kpoint = tiles_in[owner, 16:17]
         kept = [kept[k] + jnp.where(kpoint == k, tile, 0.0) for k in range(NKPT)]
-    kept = [value + pltpu.roll(value, 64, 1) for value in kept]
-    out_ref[...] = jnp.concatenate(kept, 0).T[:64]
-
+    for k in range(NKPT):
+        value = kept[k] + pltpu.roll(kept[k], 64, 1)
+        out_ref[0, k] = value[:, :32]
+        out_ref[1, k] = value[:, 32:64]
+
+    for copy in sent:
+        copy.wait_send()
     for offset in range(1, NPAIR):
-        table_copy(offset).wait_send()
         tile_copy(offset).wait_send()
     for offset in range(1, NSLAB):
         sums_copy(0, offset).wait_send()
@@ -207,30 +312,28 @@
 def local(integrals, coef_table, row_slot, pair_k):
     naux = integrals.shape[2]
     blocks = integrals.reshape(integrals.shape[1:])
-    kpoints = jnp.repeat(pair_k.astype(BF16), 64, axis=1)
-    kpoints = jnp.broadcast_to(jnp.concatenate([kpoints, kpoints], 1), (PIECE - ROWS, NORB))
-    piece = jnp.concatenate([coef_table.reshape(ROWS, 2 * NOCC), kpoints], 0)
     vmem = pl.BlockSpec(memory_space=pltpu.VMEM)
     out = pl.pallas_call(
         kernel,
-        out_shape=jax.ShapeDtypeStruct((64, ROWS), F32),
+        out_shape=jax.ShapeDtypeStruct((2, NKPT, 16, 32), F32),
         in_specs=[pl.BlockSpec(memory_space=pltpu.SMEM), vmem, vmem, pl.BlockSpec(memory_space=pl.ANY)],
         out_specs=vmem,
         scratch_shapes=[
             pltpu.VMEM((2, naux, NORB, NORB), BF16),
-            pltpu.VMEM((NPAIR, PIECE, NORB), BF16),
-            pltpu.VMEM((2 * NORB, NORB), F32),
+            pltpu.VMEM((NPAIR, HALVES, ROWS, ROWS), BF16),
+            pltpu.VMEM((4 * NORB, ROWS), jnp.int32),
+            pltpu.VMEM((4 * NORB, ROWS), F32),
             pltpu.VMEM((NORB, 2 * NORB), BF16),
             pltpu.VMEM((2 * NORB, NORB), BF16),
             pltpu.VMEM((NORB, NORB), F32),
             pltpu.VMEM((NORB, NORB), F32),
             pltpu.VMEM((2, NSLAB, ROWS, ROWS), F32),
             pltpu.VMEM((2, NSLAB, ROWS, ROWS), F32),
-            pltpu.VMEM((NORB, ROWS), F32),
-            pltpu.VMEM((NPAIR, 16, ROWS), F32),
+            pltpu.VMEM((NPAIR, 24, ROWS), F32),
+            pltpu.VMEM((NPAIR, 24, ROWS), F32),
             pltpu.SemaphoreType.DMA((CHUNKS,)),
-            pltpu.SemaphoreType.DMA((NPAIR,)),
-            pltpu.SemaphoreType.DMA((NPAIR,)),
+            pltpu.SemaphoreType.DMA((30,)),
+            pltpu.SemaphoreType.DMA((30,)),
             pltpu.SemaphoreType.DMA((2, NSLAB)),
             pltpu.SemaphoreType.DMA((2, NSLAB)),
             pltpu.SemaphoreType.DMA((NPAIR,)),
@@ -238,8 +341,8 @@
         ],
         compiler_params=pltpu.CompilerParams(
             collective_id=0, has_side_effects=True, vmem_limit_bytes=56 * 2**20),
-    )(pair_k, piece, row_slot.reshape(16, ROWS), blocks)
-    return out.reshape(2, 32, NKPT, 16).transpose(0, 2, 1, 3)
+    )(pair_k, coef_table.reshape(HALVES, ROWS, ROWS), row_slot.reshape(16, ROWS), blocks)
+    return out.transpose(0, 1, 3, 2)
 
 
 def solution(mesh):

time: 66.8 us -> 55.9 us (0.84)
  Pallas kernels: 62.5 us -> 54.2 us
  other arithmetic: 1.32 us -> 0 us
  local copies, waits for them, and re-layouts: 2.66 us -> 1.57 us
    pallas_call x1, Pallas kernels: 62.5 us -> 54.2 us  [local(): pl.pallas_call(kernel, out_shape=jax.ShapeDtypeStruct((2, NKPT, 16, 32),...]
    pallas_call x1 -> x0, local copies, waits for them, and re-layouts: 0.85 us -> none  [local(): pl.pallas_call(kernel, out_shape=jax.ShapeDtypeStruct((64, ROWS), F32), i...]
    unnamed x1, local copies, waits for them, and re-layouts: 0.85 us -> 1.57 us
where the time goes in v2:
time: 55.9 us; the launch traced here: 55.8 us
  Pallas kernels  54.2 us (97%)
  local copies, waits for them, and re-layouts  1.57 us (3%)
    pallas_call x1, Pallas kernels, local(): pl.pallas_call(kernel, out_shape=jax.ShapeDtypeStruct((2, NKPT, 16, 32),...  54.2 us
    unnamed x1, local copies, waits for them, and re-layouts  1.57 us

profile of v2, /device:TPU:1, one launch (start us, length us, event | category | flops | bytes accessed | tf_op | source)
XLA Modules:
  0.0 55.8 jit_solution(8137804734122909455)
XLA Ops:
  0.0 54.2 %shard_map.46 = f32[2,8,16,32]{3,2,1,0:T(8,128)} custom-call(s32[1,2]{1,0:T(1,128)} %pair_ref.1, bf16[2,128,128]{2,1,0:T(8,128)(2,1)} %bitcast.6, s32[16,128]{1,0:T(8,128)} %bitcast.7, bf16[2,64,256,256]{3,2,1,0:T(8,128)(2,1)} %bitcast.4), custom_call_target="tpu_custom_call" | custom-call | tf_op jit(solution)/shard_map/pallas_call | solution.py:316
  54.2 1.6 %copy.6 = f32[2,8,32,16]{2,3,1,0:T(8,128)} copy(f32[2,8,32,16]{2,3,1,0:T(8,128)} %bitcast.5) | data formatting | bytes 65536

commit v3 on v1

v3 whole, which is shorter than its diff:
```python
import jax
import jax.numpy as jnp
from jax import lax
from jax.experimental import pallas as pl
from jax.experimental.pallas import tpu as pltpu
from jax.sharding import PartitionSpec as P

NKPT = 8
NORB = 256
NOCC = 128
NPAIR = 16
NSLAB = 8
ROWS = 128
HALVES = 2
GROUP = 16
CHUNKS = 16
F32 = jnp.float32
BF16 = jnp.bfloat16
MESH = pl.DeviceIdType.MESH


def product(left, right):
    return lax.dot_general(left, right, (((1,), (0,)), ((), ())), preferred_element_type=F32)


def product_nt(left, right):
    return lax.dot_general(left, right, (((1,), (1,)), ((), ())), preferred_element_type=F32)


def product_tn(left, right):
    return lax.dot_general(left, right, (((0,), (0,)), ((), ())), preferred_element_type=F32)


def places(me, slab):
    x, low, core = me // 4, me // 2 % 2, me % 2
    y, high = slab // 2, slab % 2
    beyond = (y * 2 + lax.rem(high + low, 2), y * 2 + lax.rem(high + 1 - low, 2))

    def place(dx, dz=0, way=0):
        pair = lax.rem(x + dx, 4) * 4 + (1 - low if dz else low) * 2 + core
        return pair, (beyond[way] if dz else slab)

    return place


def kernel(pair_hbm, piece_hbm, slot_hbm, blocks_ref, out_ref, pair_ref, slot_ref, blocks, table, offsets, picked,
           second_w, first_w, kept, kept_turned, k_real, k_cross, sums_out, sums_in, tiles_out, tiles_in,
           load_sem, table_send, table_recv, sums_send, sums_recv, tiles_send, tiles_recv):
    me = lax.axis_index("pair")
    slab = lax.axis_index("aux")
    naux = blocks.shape[1]
    step = naux // CHUNKS
    factor = 1.0 / (naux * NSLAB * NOCC)
    place = places(me, slab)
    core = me % 2
    partner = (me + 1 - 2 * core, slab)

    def load(chunk):
        span = pl.ds(chunk * step, step)
        return pltpu.make_async_copy(blocks_ref.at[:, span], blocks.at[:, span], load_sem.at[chunk])

    barrier = pltpu.get_barrier_semaphore()
    beyond = (slab // 2) * 2 + 1 - slab % 2
    greeted = [(place(dx, 1)[0], beyond) for dx in range(4)]
    greeted += [(lax.rem(me + offset, NPAIR), slab) for offset in range(1, NPAIR)]
    greeted += [(me, lax.rem(slab + offset, NSLAB)) for offset in range(1, NSLAB)]
    for peer in greeted:
        pl.semaphore_signal(barrier, inc=1, device_id=peer, device_id_type=MESH)

    small = [pltpu.make_async_copy(pair_hbm, pair_ref, load_sem.at[CHUNKS]),
             pltpu.make_async_copy(slot_hbm, slot_ref, load_sem.at[CHUNKS + 1]),
             pltpu.make_async_copy(piece_hbm, table.at[me], load_sem.at[CHUNKS + 2])]
    for copy in small:
        copy.start()
    for copy in small:
        copy.wait()

    first_k = pair_ref[0, 0]
    second_k = pair_ref[0, 1]
    slots = slot_ref[...]
    lane = lax.broadcasted_iota(jnp.int32, (ROWS, ROWS), 1)
    for at, kpoint in enumerate((second_k, first_k)):
        for half in range(2):
            row = jnp.zeros((1, ROWS), jnp.int32)
            for k in range(NKPT):
                row = jnp.where(kpoint == k, slots[2 * k + half:2 * k + half + 1], row)
            where = 2 * jnp.broadcast_to(row, (ROWS, ROWS)).T - lane
            for part in range(2):
                begin = (at * 4 + part * 2 + half) * ROWS
                offsets[begin:begin + ROWS] = where + part

    pl.semaphore_wait(barrier, len(greeted))

    sources = [(0, 1), (1, 0), (3, 0), (1, 1), (3, 1), (2, 0), (2, 1)]

    def owner_of(dx, dz):
        return place(4 - dx, dz)[0]

    def table_copy(source, half):
        at = sources.index(source) * HALVES + half
        return pltpu.make_async_remote_copy(
            src_ref=table.at[me, half], dst_ref=table.at[me, half],
            send_sem=table_send.at[at], recv_sem=table_recv.at[at],
            device_id=place(*source, half), device_id_type=MESH)

    def core_copy(source, half):
        at = (len(sources) if source is None else sources.index(source)) * HALVES + half + 14
        slot = me if source is None else owner_of(*source)
        return pltpu.make_async_remote_copy(
            src_ref=table.at[slot, half], dst_ref=table.at[slot, half],
            send_sem=table_send.at[at], recv_sem=table_recv.at[at],
            device_id=partner, device_id_type=MESH)

    def pick(slot):
        rows = table[slot].reshape(2 * ROWS, ROWS)
        base = slot * (2 * ROWS)
        hot = [jnp.where(offsets[...] == base + half * ROWS, 1.0, 0.0).astype(BF16) for half in range(HALVES)]
        return product(jnp.concatenate(hot, 1), rows)

    def other(slot):
        return slot + 1 - 2 * core

    for source in sources:
        for half in range(HALVES):
            table_copy(source, half).start()
    for half in range(HALVES):
        core_copy(None, half).start()
    for chunk in range(CHUNKS):
        load(chunk).start()
    picked[...] = pick(me)
    for half in range(HALVES):
        core_copy(None, half).wait_recv()
    picked[...] += pick(other(me))
    for source in sources:
        for half in range(HALVES):
            table_copy(source, half).wait_recv()
            core_copy(source, half).start()
        picked[...] += pick(owner_of(*source))
        at = sources.index(source)
        if at:
            for half in range(HALVES):
                core_copy(sources[at - 1], half).wait_recv()
            picked[...] += pick(other(owner_of(*sources[at - 1])))
    for half in range(HALVES):
        core_copy(sources[-1], half).wait_recv()
    picked[...] += pick(other(owner_of(*sources[-1])))

    parts = [picked[begin:begin + NORB] for begin in range(0, 4 * NORB, NORB)]
    real, imag = parts[:2]
    second_w[...] = jnp.concatenate(
        [jnp.concatenate([real, imag], 1), jnp.concatenate([-imag, real], 1)], 0).astype(BF16)
    real, imag = parts[2:]
    first_w[...] = jnp.concatenate(
        [jnp.concatenate([real, imag], 1).T, jnp.concatenate([imag, -real], 1).T], 1).astype(BF16)

    def sums_copy(block, part, offset):
        peer = lax.rem(slab + offset, NSLAB)
        return pltpu.make_async_remote_copy(
            src_ref=sums_out.at[block, part, peer], dst_ref=sums_in.at[block, part, slab],
            send_sem=sums_send.at[block, part, offset], recv_sem=sums_recv.at[block, part, offset],
            device_id=(me, peer), device_id_type=MESH)

    def clear():
        k_real[...] = jnp.zeros_like(k_real)
        k_cross[...] = jnp.zeros_like(k_cross)

    at = lax.broadcasted_iota(jnp.int32, (64, ROWS), 1)

    def send_sums(block, part):
        value = k_cross[...].T - k_cross[...] if part else k_real[...]
        value = (value * factor).reshape(8, 4, 8, NORB)
        for peer in range(NSLAB):
            tile, shift = peer // 4, peer % 4
            message = None
            for b in range(4):
                rows = value[:, b, :, tile * ROWS:(tile + 1) * ROWS].reshape(64, ROWS)
                turn = (b - shift) % 4 * 32
                if turn:
                    rows = pltpu.roll(rows, turn, 1)
                message = rows if message is None else jnp.where(at >= b * 32, rows, message)
            sums_out[block, part, peer] = message
        for offset in range(1, NSLAB):
            sums_copy(block, part, offset).start()

    clear()

    def left(group, carry):
        for chunk in range(GROUP // step):
            load(group * (GROUP // step) + chunk).wait()
        rounded = []
        for p in range(GROUP):
            both = jnp.concatenate([blocks[0, group * GROUP + p], blocks[1, group * GROUP + p]], 1)
            rounded.append(product(both, second_w[...]).astype(BF16))
        real = jnp.concatenate([x[:, :NOCC] for x in rounded], 1)
        imag = jnp.concatenate([x[:, NOCC:] for x in rounded], 1)
        terms = product_nt(jnp.concatenate([real, imag], 0), real)
        k_real[...] += terms[:NORB] + product_nt(imag, imag)
        k_cross[...] += terms[NORB:]
        return carry

    lax.fori_loop(0, naux // GROUP, left, 0)
    send_sums(0, 0)
    send_sums(0, 1)
    clear()

    def right(group, carry):
        rounded = []
        for p in range(GROUP):
            both = jnp.concatenate([blocks[0, group * GROUP + p], blocks[1, group * GROUP + p]], 0)
            rounded.append(product(first_w[...], both).astype(BF16))
        real = jnp.concatenate([x[:NOCC] for x in rounded], 0)
        imag = jnp.concatenate([x[NOCC:] for x in rounded], 0)
        turned = imag.T
        k_cross[...] += product(turned, real)
        kept[group, 0] = real
        kept[group, 1] = imag
        kept_turned[group, 0] = real.T
        kept_turned[group, 1] = turned
        return carry

    lax.fori_loop(0, naux // GROUP, right, 0)
    send_sums(1, 1)
    real = jnp.concatenate([kept[group, part] for group in range(naux // GROUP) for part in range(2)], 0)
    turned = jnp.concatenate([kept_turned[group, part] for group in range(naux // GROUP) for part in range(2)], 1)
    k_real[...] = product(turned, real)
    send_sums(1, 0)

    def total(block, part):
        sums_in[block, part, slab] = sums_out[block, part, slab]
        for offset in range(1, NSLAB):
            sums_copy(block, part, offset).wait_recv()
        value = sums_in[block, part, 0]
        for sender in range(1, NSLAB):
            value = value + sums_in[block, part, sender]
        return value

    def tile_copy(block, offset):
        peer = lax.rem(me + offset, NPAIR)
        begin, rows = (0, 16) if block == 0 else (16, 8)
        return pltpu.make_async_remote_copy(
            src_ref=tiles_out.at[peer, pl.ds(begin, rows)], dst_ref=tiles_in.at[me, pl.ds(begin, rows)],
            send_sem=tiles_send.at[block, offset], recv_sem=tiles_recv.at[block, offset],
            device_id=(peer, slab), device_id_type=MESH)

    low = at < 64
    row = lax.broadcasted_iota(jnp.int32, (8, ROWS), 0)
    tiles_out[:, 8:16] = jnp.broadcast_to(jnp.where(row == 0, first_k, second_k).astype(F32), (NPAIR, 8, ROWS))
    for block in range(2):
        parts = [None, None]
        for part in ((0, 1) if block == 0 else (1, 0)):
            parts[part] = total(block, part)
        real, imag = parts
        even = jnp.where(low, real, pltpu.roll(imag, 64, 1)).reshape(8, 8, ROWS)
        odd = jnp.where(low, pltpu.roll(real, 64, 1), imag).reshape(8, 8, ROWS)
        begin = block * 16
        for pair in range(NPAIR):
            tiles_out[pair, begin:begin + 8] = (odd if pair % 2 else even)[pair // 2]
        for offset in range(1, NPAIR):
            tile_copy(block, offset).start()
    tiles_in[me] = tiles_out[me]
    bins = [jnp.zeros((8, ROWS), F32) for k in range(NKPT)]
    for block in range(2):
        for offset in range(1, NPAIR):
            tile_copy(block, offset).wait_recv()
        for owner in range(NPAIR):
            tile = tiles_in[owner, block * 16:block * 16 + 8]
            kpoint = tiles_in[owner, 8 + block:9 + block]
            bins = [bins[k] + jnp.where(kpoint == k, tile, 0.0) for k in range(NKPT)]
    for k in range(NKPT):
        for part in range(2):
            for upper in range(2):
                begin = part * 64 + upper * 32
                out_ref[part, k, upper * 8:upper * 8 + 8] = bins[k][:, begin:begin + 32]

    for half in range(HALVES):
        core_copy(None, half).wait_send()
        for source in sources:
            table_copy(source, half).wait_send()
            core_copy(source, half).wait_send()
    for block in range(2):
        for offset in range(1, NPAIR):
            tile_copy(block, offset).wait_send()
        for part in range(2):
            for offset in range(1, NSLAB):
                sums_copy(block, part, offset).wait_send()


def local(integrals, coef_table, row_slot, pair_k):
    naux = integrals.shape[2]
    blocks = integrals.reshape(integrals.shape[1:])
    out = pl.pallas_call(
        kernel,
        out_shape=jax.ShapeDtypeStruct((2, NKPT, 16, 32), F32),
        in_specs=[pl.BlockSpec(memory_space=pl.ANY)] * 4,
        out_specs=pl.BlockSpec(memory_space=pltpu.VMEM),
        scratch_shapes=[
            pltpu.SMEM((1, 2), jnp.int32),
            pltpu.VMEM((16, ROWS), jnp.int32),
            pltpu.VMEM((2, naux, NORB, NORB), BF16),
            pltpu.VMEM((NPAIR, HALVES, ROWS, ROWS), BF16),
            pltpu.VMEM((4 * NORB, ROWS), jnp.int32),
            pltpu.VMEM((4 * NORB, ROWS), F32),
            pltpu.VMEM((2 * NORB, NORB), BF16),
            pltpu.VMEM((NORB, 2 * NORB), BF16),
            pltpu.VMEM((naux // GROUP, 2, GROUP * NOCC, NORB), BF16),
            pltpu.VMEM((naux // GROUP, 2, NORB, GROUP * NOCC), BF16),
            pltpu.VMEM((NORB, NORB), F32),
            pltpu.VMEM((NORB, NORB), F32),
            pltpu.VMEM((2, 2, NSLAB, 64, ROWS), F32),
            pltpu.VMEM((2, 2, NSLAB, 64, ROWS), F32),
            pltpu.VMEM((NPAIR, 24, ROWS), F32),
            pltpu.VMEM((NPAIR, 24, ROWS), F32),
            pltpu.SemaphoreType.DMA((CHUNKS + 3,)),
            pltpu.SemaphoreType.DMA((30,)),
            pltpu.SemaphoreType.DMA((30,)),
            pltpu.SemaphoreType.DMA((2, 2, NSLAB)),
            pltpu.SemaphoreType.DMA((2, 2, NSLAB)),
            pltpu.SemaphoreType.DMA((2, NPAIR)),
            pltpu.SemaphoreType.DMA((2, NPAIR)),
        ],
        compiler_params=pltpu.CompilerParams(
            collective_id=0, has_side_effects=True, vmem_limit_bytes=56 * 2**20),
    )(pair_k, coef_table.reshape(HALVES, ROWS, ROWS), row_slot.reshape(16, ROWS), blocks)
    return out.transpose(0, 1, 3, 2)


def solution(mesh):
    in_specs = (P("pair", None, "aux", None, None), P("pair", None, None), P(), P("pair", None))
    out_specs = P(None, None, "aux", "pair")
    return jax.shard_map(local, mesh=mesh, in_specs=in_specs, out_specs=out_specs, check_vma=False)
```

time: 66.8 us -> 54.1 us (0.81)
  Pallas kernels: 62.5 us -> 52.4 us
  other arithmetic: 1.32 us -> 0 us
  local copies, waits for them, and re-layouts: 2.66 us -> 1.57 us
    pallas_call x1, Pallas kernels: 62.5 us -> 52.4 us  [local(): pl.pallas_call(kernel, out_shape=jax.ShapeDtypeStruct((2, NKPT, 16, 32),...]
    pallas_call x1 -> x0, local copies, waits for them, and re-layouts: 0.85 us -> none  [local(): pl.pallas_call(kernel, out_shape=jax.ShapeDtypeStruct((64, ROWS), F32), i...]
    unnamed x1, local copies, waits for them, and re-layouts: 0.85 us -> 1.57 us
where the time goes in v3:
time: 54.1 us; the launch traced here: 54 us
  Pallas kernels  52.4 us (97%)
  local copies, waits for them, and re-layouts  1.57 us (3%)
    pallas_call x1, Pallas kernels, local(): pl.pallas_call(kernel, out_shape=jax.ShapeDtypeStruct((2, NKPT, 16, 32),...  52.4 us
    unnamed x1, local copies, waits for them, and re-layouts  1.57 us

profile of v3, /device:TPU:1, one launch (start us, length us, event | category | flops | bytes accessed | tf_op | source)
XLA Modules:
  0.0 54.0 jit_solution(7754632602794326633)
XLA Ops:
  0.0 52.4 %shard_map.46 = f32[2,8,16,32]{3,2,1,0:T(8,128)} custom-call(s32[1,2]{1,0:T(1,128)} %pair_hbm.1, bf16[2,128,128]{2,1,0:T(8,128)(2,1)} %bitcast.6, s32[16,128]{1,0:T(8,128)} %bitcast.7, bf16[2,64,256,256]{3,2,1,0:T(8,128)(2,1)} %bitcast.4), custom_call_target="tpu_custom_call" | custom-call | tf_op jit(solution)/shard_map/pallas_call | solution.py:291
  52.4 1.6 %copy.6 = f32[2,8,32,16]{2,3,1,0:T(8,128)} copy(f32[2,8,32,16]{2,3,1,0:T(8,128)} %bitcast.5) | data formatting | bytes 65536

commit v4 on v3

--- a/solution.py
+++ b/solution.py
@@ -17,6 +17,8 @@
 F32 = jnp.float32
 BF16 = jnp.bfloat16
 MESH = pl.DeviceIdType.MESH
+SUM_ORDER = ((2, 1), (1, 1), (3, 1), (2, 0), (0, 1), (1, 0), (3, 0))
+TILE_ORDER = tuple((dx, dz, dc) for dx, dz in ((2, 1), (2, 0), (1, 1), (3, 1), (0, 1), (1, 0), (3, 0)) for dc in (0, 1)) + ((0, 0, 1),)
 
 
 def product(left, right):
@@ -154,7 +156,8 @@
         [jnp.concatenate([real, imag], 1).T, jnp.concatenate([imag, -real], 1).T], 1).astype(BF16)
 
     def sums_copy(block, part, offset):
-        peer = lax.rem(slab + offset, NSLAB)
+        dy, dz = SUM_ORDER[offset - 1]
+        peer = lax.rem(slab // 2 + dy, 4) * 2 + lax.rem(slab % 2 + dz, 2)
         return pltpu.make_async_remote_copy(
             src_ref=sums_out.at[block, part, peer], dst_ref=sums_in.at[block, part, slab],
             send_sem=sums_send.at[block, part, offset], recv_sem=sums_recv.at[block, part, offset],
@@ -218,7 +221,7 @@
         kept_turned[group, 1] = turned
         return carry
 
-    lax.fori_loop(0, naux // GROUP, right, 0)
+    lax.fori_loop(0, naux // GROUP, right, 0, unroll=2)
     send_sums(1, 1)
     real = jnp.concatenate([kept[group, part] for group in range(naux // GROUP) for part in range(2)], 0)
     turned = jnp.concatenate([kept_turned[group, part] for group in range(naux // GROUP) for part in range(2)], 1)
@@ -235,7 +238,8 @@
         return value
 
     def tile_copy(block, offset):
-        peer = lax.rem(me + offset, NPAIR)
+        dx, dz, dc = TILE_ORDER[offset - 1]
+        peer = lax.rem(me // 4 + dx, 4) * 4 + lax.rem(me // 2 % 2 + dz, 2) * 2 + lax.rem(core + dc, 2)
         begin, rows = (0, 16) if block == 0 else (16, 8)
         return pltpu.make_async_remote_copy(
             src_ref=tiles_out.at[peer, pl.ds(begin, rows)], dst_ref=tiles_in.at[me, pl.ds(begin, rows)],

time: 54.1 us -> 52.8 us (0.976)
  Pallas kernels: 52.4 us -> 51 us
    pallas_call x1, Pallas kernels: 52.4 us -> 51 us  [local(): pl.pallas_call(kernel, out_shape=jax.ShapeDtypeStruct((2, NKPT, 16, 32),...]
where the time goes in v4:
time: 52.8 us; the launch traced here: 52.6 us
  Pallas kernels  51 us (97%)
  local copies, waits for them, and re-layouts  1.57 us (3%)
    pallas_call x1, Pallas kernels, local(): pl.pallas_call(kernel, out_shape=jax.ShapeDtypeStruct((2, NKPT, 16, 32),...  51 us
    unnamed x1, local copies, waits for them, and re-layouts  1.57 us

profile of v4, /device:TPU:1, one launch (start us, length us, event | category | flops | bytes accessed | tf_op | source)
XLA Modules:
  0.0 52.6 jit_solution(3029299567376686861)
XLA Ops:
  0.0 51.0 %shard_map.46 = f32[2,8,16,32]{3,2,1,0:T(8,128)} custom-call(s32[1,2]{1,0:T(1,128)} %pair_hbm.1, bf16[2,128,128]{2,1,0:T(8,128)(2,1)} %bitcast.6, s32[16,128]{1,0:T(8,128)} %bitcast.7, bf16[2,64,256,256]{3,2,1,0:T(8,128)(2,1)} %bitcast.4), custom_call_target="tpu_custom_call" | custom-call | tf_op jit(solution)/shard_map/pallas_call | solution.py:295
  51.0 1.6 %copy.6 = f32[2,8,32,16]{2,3,1,0:T(8,128)} copy(f32[2,8,32,16]{2,3,1,0:T(8,128)} %bitcast.5) | data formatting | bytes 65536

commit v5 on v4

--- a/solution.py
+++ b/solution.py
@@ -13,7 +13,7 @@
 ROWS = 128
 HALVES = 2
 GROUP = 16
-CHUNKS = 16
+CHUNKS = 8
 F32 = jnp.float32
 BF16 = jnp.bfloat16
 MESH = pl.DeviceIdType.MESH
@@ -76,6 +76,8 @@
         copy.start()
     for copy in small:
         copy.wait()
+    for chunk in range(CHUNKS):
+        load(chunk).start()
 
     first_k = pair_ref[0, 0]
     second_k = pair_ref[0, 1]
@@ -127,8 +129,6 @@
             table_copy(source, half).start()
     for half in range(HALVES):
         core_copy(None, half).start()
-    for chunk in range(CHUNKS):
-        load(chunk).start()
     picked[...] = pick(me)
     for half in range(HALVES):
         core_copy(None, half).wait_recv()

time: 52.8 us -> 52.7 us (level)
  no operation moved by 1% of the time
where the time goes in v5:
time: 52.7 us; the launch traced here: 52.5 us
  Pallas kernels  50.9 us (97%)
  local copies, waits for them, and re-layouts  1.57 us (3%)
    pallas_call x1, Pallas kernels, local(): pl.pallas_call(kernel, out_shape=jax.ShapeDtypeStruct((2, NKPT, 16, 32),...  50.9 us
    unnamed x1, local copies, waits for them, and re-layouts  1.57 us

profile of v5, /device:TPU:1, one launch (start us, length us, event | category | flops | bytes accessed | tf_op | source)
XLA Modules:
  0.0 52.5 jit_solution(13049712436797352660)
XLA Ops:
  0.0 50.9 %shard_map.46 = f32[2,8,16,32]{3,2,1,0:T(8,128)} custom-call(s32[1,2]{1,0:T(1,128)} %pair_hbm.1, bf16[2,128,128]{2,1,0:T(8,128)(2,1)} %bitcast.6, s32[16,128]{1,0:T(8,128)} %bitcast.7, bf16[2,64,256,256]{3,2,1,0:T(8,128)(2,1)} %bitcast.4), custom_call_target="tpu_custom_call" | custom-call | tf_op jit(solution)/shard_map/pallas_call | solution.py:295
  50.9 1.6 %copy.6 = f32[2,8,32,16]{2,3,1,0:T(8,128)} copy(f32[2,8,32,16]{2,3,1,0:T(8,128)} %bitcast.5) | data formatting | bytes 65536
